TPU v7x, 256 devices: a whole 4x4x8 slice. The times are simulated.
256 devices in a mesh: corpus: 64 (over y, z, x_hi), vocab: 4 (over x_lo, core).
Axes of the slice: x: 4 (x_hi: 2, x_lo: 2; x = x_hi * 2 + x_lo), y: 4, z: 8, core: 2. Of those that a mesh axis runs over, the one named last changes fastest.
Arguments:
- eval_tiles: bfloat16 [64, 12, 128, 512], P('corpus', 'vocab'), may hold values from 0.019897461 to 2
- eval_tile_list: int32 [64, 12], P(None, 'vocab'), may hold values from 0 to 128, as said below
- corpus_tiles: bfloat16 [256, 12, 128, 512], P('corpus', 'vocab'), may hold values from 0.019897461 to 2
- corpus_tile_list: int32 [256, 12], P('corpus', 'vocab'), may hold values from 0 to 128, as said below
- pair_eval_block: int32 [6144], P('corpus'), may hold values from 0 to 63
- pair_corpus_block: int32 [6144], P('corpus'), may hold values from 0 to 3
- pair_count: int32 [64], P('corpus'), may hold values from 12 to 96, as said below
- eval_norm: float32 [8192], replicated, may hold values from 8 to 32
- corpus_norm: float32 [32768], P('corpus'), may hold values from 8 to 32
Outputs:
- cosine_tiles: float32 [6144, 128, 128], P(('corpus', 'vocab'))
Inputs may be any that keep to these rules, and one draw needn't show every extreme that they name: `eval_tile_list`: value 128 marks an empty slot; other ids of one row block in one slice are distinct. Slot 0 of a block and slice is never empty. `corpus_tile_list`: value 128 marks an empty slot; other ids of one row block in one slice are distinct. Slot 0 of a block and slice is never empty. Shard c's live pair slots are its first pair_count[c] slots. Some shard is full.
All inputs are finite; a program needn't handle non-finite values.
Results may differ from a plain program's by a relative error of at most 0.0003.
Values may be sent and summed in bfloat16 or wider, within the bound.
A program may use at most 128 MiB of HBM per device.

v0:
```python
import jax
import jax.numpy as jnp
from jax import lax
from jax.sharding import PartitionSpec as P

VOCAB = 262144
GROUP = 8


def local(
    eval_tiles,
    eval_tile_list,
    corpus_tiles,
    corpus_tile_list,
    pair_eval_block,
    pair_corpus_block,
    pair_count,
    eval_norm,
    corpus_norm,
):
    slices = lax.axis_size("vocab")
    term_width = corpus_tiles.shape[3]
    tile_rows = corpus_tiles.shape[2]
    tiles_slice = VOCAB // (term_width * slices)
    pair_slots = pair_eval_block.shape[0]
    quarter = pair_slots // slices
    every_eval = lax.all_gather(eval_tiles, "corpus", axis=0, tiled=True)
    position = jnp.arange(pair_slots, dtype=jnp.int32)
    own_live = position < pair_count[0]
    groups = quarter * lax.axis_size("vocab") // GROUP

    def one_group(group_index, totals):
        first_slot = group_index * GROUP
        living = lax.dynamic_slice_in_dim(own_live, first_slot, GROUP)

        def compute(current):
            eval_index = lax.dynamic_slice_in_dim(pair_eval_block, first_slot, GROUP)
            block_index = lax.dynamic_slice_in_dim(pair_corpus_block, first_slot, GROUP)
            eval_part = every_eval[eval_index]
            eval_list = eval_tile_list[eval_index]
            corpus_part = corpus_tiles[block_index]
            corpus_list = corpus_tile_list[block_index]
            matched = (eval_list[:, :, None] == corpus_list[:, None, :]) & (
                eval_list[:, :, None] < tiles_slice
            )
            aligned = jnp.einsum(
                "gij,gjrt->girt",
                matched.astype(jnp.bfloat16),
                corpus_part,
                preferred_element_type=jnp.float32,
            ).astype(jnp.bfloat16)
            products = jnp.einsum(
                "girt,gist->grs", eval_part, aligned, preferred_element_type=jnp.float32
            )
            products = jnp.where(living[:, None, None], products, 0.0)
            return lax.dynamic_update_slice_in_dim(current, products, group_index * GROUP, 0)

        return lax.cond(jnp.any(living), compute, lambda current: current, totals)

    start_totals = jnp.zeros((quarter * lax.axis_size("vocab"), tile_rows, tile_rows), jnp.float32)
    summed = lax.psum_scatter(
        lax.fori_loop(0, groups, one_group, start_totals), "vocab", scatter_dimension=0, tiled=True
    )
    vocab_index = lax.axis_index("vocab")
    first_pair = vocab_index * quarter
    mine_eval = lax.dynamic_slice_in_dim(pair_eval_block, first_pair, quarter)
    mine_block = lax.dynamic_slice_in_dim(pair_corpus_block, first_pair, quarter)
    mine_live = lax.dynamic_slice_in_dim(own_live, first_pair, quarter)
    eval_scale = eval_norm.reshape(-1, tile_rows)[mine_eval]
    corpus_scale = corpus_norm.reshape(-1, tile_rows)[mine_block]
    cosine = summed / (eval_scale[:, :, None] * corpus_scale[:, None, :])
    return jnp.where(mine_live[:, None, None], cosine, 0.0)


def solution(mesh):
    in_specs = (
        P("corpus", "vocab", None, None),
        P(None, "vocab"),
        P("corpus", "vocab", None, None),
        P("corpus", "vocab"),
        P("corpus"),
        P("corpus"),
        P("corpus"),
        P(),
        P("corpus"),
    )
    out_specs = P(("corpus", "vocab"), None, None)
    return jax.shard_map(local, mesh=mesh, in_specs=in_specs, out_specs=out_specs, check_vma=False)
```

profile of v0, /device:TPU:1, one launch (start us, length us, event | category | flops | bytes accessed | tf_op | source)
XLA Modules:
  0.0 635.2 jit_solution(17635871114623681145)
XLA Ops:
  6.5 0.7 all-gather.2.cloned.1.call-update
  8.0 0.8 copy.11
  8.8 279.0 %all-gather.2.cloned.1.call-done = bf16[64,3,128,512]{3,2,1,0:T(8,128)(2,1)} async-done(((bf16[1,3,128,512]{3,2,1,0:T(8,128)(2,1)}), bf16[64,3,128,512]{3,2,1,0:T(8,128)(2,1)}) %all-gather.2.cloned.1.call-update) | async-done | bytes 25165840 | tf_op jit(solution)/shard_map/all_gather | solution.py:27
  287.8 3.5 broadcast_in_dim.49
  291.3 145.8 %while.16 = (s32[]{:T(128)}, f32[96,128,128]{2,1,0:T(8,128)}, pred[96]{0:T(512)(128)(4,1)S(1)}, s32[96]{0:T(128)S(1)}, bf16[64,3,128,512]{3,2,1,0:T(8,128)(2,1)}...) while((s32[]{:T(128)}, f32[96,128,128]{2,1,0:T(8,128)}, ...), condition=%wide.region_4.5_spmd, body=%wide.region_0.4_spmd.sunk | while | flops 412223712 | bytes 38282672 | solution.py:62
  291.3 0.8 fusion.15
  292.8 21.3 %conditional.2 = (f32[96,128,128]{2,1,0:T(8,128)}) conditional(s32[]{:T(128)} %convert_element_type.20, f32[96,128,128]{2,1,0:T(8,128)} %get-tuple-element.313, (pred[8]{0:T(512)(128)(4,1)S(1)}, s32[]{:T(128)}, s32[96]{0:T(128)S(1)}, bf16[64,3,128,512]{3,2,1,0:T(8,128)(2,1)}, s32[64,3]{1,0:T(8,128)S(1)}, /*index=5*/s32[96]{0:T(128)S(1)}, ...), branch_computations={%region_2.0_spmd, %region_3.3_spmd} | conditional | flops 412223712 | bytes 38282388 | solution.py:58
  292.9 10.5 %gather_fusion = bf16[8,3,128,512]{3,2,1,0:T(8,128)(2,1)} fusion(bf16[64,3,128,512]{3,2,1,0:T(8,128)(2,1)} %get-tuple-element.178, s32[1024]{0:T(1024)S(1)} %pad_clamp_fusion.1), kind=kCustom, calls=%fused_computation | custom fusion | bytes 6291488 | tf_op jit(solution)/shard_map/while/body/eval_jaxpr/cond/branch_1_fun/gather | solution.py:39
  303.4 2.5 gather_fusion.3
  305.9 0.6 gather_fusion.2
  306.5 0.6 gather_fusion.1
  307.1 4.9 fusion
  312.0 2.1 fusion.5
  314.1 0.8 fusion.15
  315.6 21.3 %conditional.2 = (f32[96,128,128]{2,1,0:T(8,128)}) conditional(s32[]{:T(128)} %convert_element_type.20, f32[96,128,128]{2,1,0:T(8,128)} %get-tuple-element.313, (pred[8]{0:T(512)(128)(4,1)S(1)}, s32[]{:T(128)}, s32[96]{0:T(128)S(1)}, bf16[64,3,128,512]{3,2,1,0:T(8,128)(2,1)}, s32[64,3]{1,0:T(8,128)S(1)}, /*index=5*/s32[96]{0:T(128)S(1)}, ...), branch_computations={%region_2.0_spmd, %region_3.3_spmd} | conditional | flops 412223712 | bytes 38282388 | solution.py:58
  315.7 10.5 %gather_fusion = bf16[8,3,128,512]{3,2,1,0:T(8,128)(2,1)} fusion(bf16[64,3,128,512]{3,2,1,0:T(8,128)(2,1)} %get-tuple-element.178, s32[1024]{0:T(1024)S(1)} %pad_clamp_fusion.1), kind=kCustom, calls=%fused_computation | custom fusion | bytes 6291488 | tf_op jit(solution)/shard_map/while/body/eval_jaxpr/cond/branch_1_fun/gather | solution.py:39
  326.2 2.5 gather_fusion.3
  328.7 0.6 gather_fusion.2
  329.3 0.6 gather_fusion.1
  329.9 4.9 fusion
  334.8 2.1 fusion.5
  336.9 0.8 fusion.15
  338.4 21.3 %conditional.2 = (f32[96,128,128]{2,1,0:T(8,128)}) conditional(s32[]{:T(128)} %convert_element_type.20, f32[96,128,128]{2,1,0:T(8,128)} %get-tuple-element.313, (pred[8]{0:T(512)(128)(4,1)S(1)}, s32[]{:T(128)}, s32[96]{0:T(128)S(1)}, bf16[64,3,128,512]{3,2,1,0:T(8,128)(2,1)}, s32[64,3]{1,0:T(8,128)S(1)}, /*index=5*/s32[96]{0:T(128)S(1)}, ...), branch_computations={%region_2.0_spmd, %region_3.3_spmd} | conditional | flops 412223712 | bytes 38282388 | solution.py:58
  338.5 10.5 %gather_fusion = bf16[8,3,128,512]{3,2,1,0:T(8,128)(2,1)} fusion(bf16[64,3,128,512]{3,2,1,0:T(8,128)(2,1)} %get-tuple-element.178, s32[1024]{0:T(1024)S(1)} %pad_clamp_fusion.1), kind=kCustom, calls=%fused_computation | custom fusion | bytes 6291488 | tf_op jit(solution)/shard_map/while/body/eval_jaxpr/cond/branch_1_fun/gather | solution.py:39
  349.0 2.5 gather_fusion.3
  351.5 0.6 gather_fusion.2
  352.1 0.6 gather_fusion.1
  352.7 4.9 fusion
  357.6 2.1 fusion.5
  359.7 0.8 fusion.15
  361.1 21.3 %conditional.2 = (f32[96,128,128]{2,1,0:T(8,128)}) conditional(s32[]{:T(128)} %convert_element_type.20, f32[96,128,128]{2,1,0:T(8,128)} %get-tuple-element.313, (pred[8]{0:T(512)(128)(4,1)S(1)}, s32[]{:T(128)}, s32[96]{0:T(128)S(1)}, bf16[64,3,128,512]{3,2,1,0:T(8,128)(2,1)}, s32[64,3]{1,0:T(8,128)S(1)}, /*index=5*/s32[96]{0:T(128)S(1)}, ...), branch_computations={%region_2.0_spmd, %region_3.3_spmd} | conditional | flops 412223712 | bytes 38282388 | solution.py:58
  361.3 10.5 %gather_fusion = bf16[8,3,128,512]{3,2,1,0:T(8,128)(2,1)} fusion(bf16[64,3,128,512]{3,2,1,0:T(8,128)(2,1)} %get-tuple-element.178, s32[1024]{0:T(1024)S(1)} %pad_clamp_fusion.1), kind=kCustom, calls=%fused_computation | custom fusion | bytes 6291488 | tf_op jit(solution)/shard_map/while/body/eval_jaxpr/cond/branch_1_fun/gather | solution.py:39
  371.8 2.5 gather_fusion.3
  374.3 0.6 gather_fusion.2
  374.9 0.6 gather_fusion.1
  375.4 4.9 fusion
  380.4 2.0 fusion.5
  382.4 0.8 fusion.15
  383.9 21.3 %conditional.2 = (f32[96,128,128]{2,1,0:T(8,128)}) conditional(s32[]{:T(128)} %convert_element_type.20, f32[96,128,128]{2,1,0:T(8,128)} %get-tuple-element.313, (pred[8]{0:T(512)(128)(4,1)S(1)}, s32[]{:T(128)}, s32[96]{0:T(128)S(1)}, bf16[64,3,128,512]{3,2,1,0:T(8,128)(2,1)}, s32[64,3]{1,0:T(8,128)S(1)}, /*index=5*/s32[96]{0:T(128)S(1)}, ...), branch_computations={%region_2.0_spmd, %region_3.3_spmd} | conditional | flops 412223712 | bytes 38282388 | solution.py:58
  384.0 10.5 %gather_fusion = bf16[8,3,128,512]{3,2,1,0:T(8,128)(2,1)} fusion(bf16[64,3,128,512]{3,2,1,0:T(8,128)(2,1)} %get-tuple-element.178, s32[1024]{0:T(1024)S(1)} %pad_clamp_fusion.1), kind=kCustom, calls=%fused_computation | custom fusion | bytes 6291488 | tf_op jit(solution)/shard_map/while/body/eval_jaxpr/cond/branch_1_fun/gather | solution.py:39
  394.6 2.5 gather_fusion.3
  397.1 0.6 gather_fusion.2
  397.6 0.6 gather_fusion.1
  398.2 4.9 fusion
  403.1 2.1 fusion.5
  405.2 0.8 fusion.15
  406.7 21.3 %conditional.2 = (f32[96,128,128]{2,1,0:T(8,128)}) conditional(s32[]{:T(128)} %convert_element_type.20, f32[96,128,128]{2,1,0:T(8,128)} %get-tuple-element.313, (pred[8]{0:T(512)(128)(4,1)S(1)}, s32[]{:T(128)}, s32[96]{0:T(128)S(1)}, bf16[64,3,128,512]{3,2,1,0:T(8,128)(2,1)}, s32[64,3]{1,0:T(8,128)S(1)}, /*index=5*/s32[96]{0:T(128)S(1)}, ...), branch_computations={%region_2.0_spmd, %region_3.3_spmd} | conditional | flops 412223712 | bytes 38282388 | solution.py:58
  406.8 10.5 %gather_fusion = bf16[8,3,128,512]{3,2,1,0:T(8,128)(2,1)} fusion(bf16[64,3,128,512]{3,2,1,0:T(8,128)(2,1)} %get-tuple-element.178, s32[1024]{0:T(1024)S(1)} %pad_clamp_fusion.1), kind=kCustom, calls=%fused_computation | custom fusion | bytes 6291488 | tf_op jit(solution)/shard_map/while/body/eval_jaxpr/cond/branch_1_fun/gather | solution.py:39
  417.3 2.5 gather_fusion.3
  419.8 0.6 gather_fusion.2
  420.4 0.6 gather_fusion.1
  421.0 4.9 fusion
  425.9 2.0 fusion.5
  428.0 0.8 fusion.15
  429.5 0.8 fusion.15
  431.0 0.8 fusion.15
  432.5 0.8 fusion.15
  434.1 0.8 fusion.15
  435.6 0.8 fusion.15
  437.3 0.5 copy-done.4
  437.8 0.6 gather_fusion.5
  438.4 0.6 gather_fusion.4
  438.9 186.3 %reduce-scatter.2.cloned.1.call-done = f32[24,128,128]{2,1,0:T(8,128)} async-done(((f32[96,128,128]{2,1,0:T(8,128)}), f32[24,128,128]{2,1,0:T(8,128)}) %reduce-scatter.2.cloned.1.call-update) | async-done | bytes 1572880 | tf_op jit(solution)/shard_map/reduce_scatter | solution.py:61
  625.3 3.1 divide_select_fusion
  (61 shorter events, 0.9 us)
Async XLA Ops:
  6.5 431.8 %copy-start = (f32[8192]{0:T(1024)S(1)}, f32[8192]{0:T(1024)}, u32[]{:S(2)}) copy-start(f32[8192]{0:T(1024)} %param.20) | copy-start | bytes 98308
  6.5 281.3 %all-gather.2.cloned.1.call-start = ((), (), s32[]{:S(2)}) async-start(), calls=%async_computation.1 | async-start | bytes 25559040 | tf_op jit(solution)/shard_map/all_gather | solution.py:27
  7.3 618.0 %reduce-scatter.2.cloned.1.call-start = ((), (), s32[]{:S(2)}) async-start(), calls=%async_computation.2 | async-start | bytes 7864320 | tf_op jit(solution)/shard_map/reduce_scatter | solution.py:61
  8.7 282.5 %copy-start.1 = (bf16[4,3,128,512]{3,2,1,0:T(8,128)(2,1)S(1)}, bf16[4,3,128,512]{3,2,1,0:T(8,128)(2,1)}, u32[]{:S(2)}) copy-start(bf16[4,3,128,512]{3,2,1,0:T(8,128)(2,1)} %param.15) | copy-start | bytes 4718596
  8.7 282.5 %copy-start.3 = (s32[4,3]{1,0:T(4,128)S(1)}, s32[4,3]{1,0:T(4,128)}, u32[]{:S(2)}) copy-start(s32[4,3]{1,0:T(4,128)} %param.16) | copy-start | bytes 148
  8.7 282.5 %copy-start.5 = (s32[96]{0:T(128)S(1)}, s32[96]{0:T(128)}, u32[]{:S(2)}) copy-start(s32[96]{0:T(128)} %param.17) | copy-start | bytes 1156
  8.8 282.5 %copy-start.6 = (s32[96]{0:T(128)S(1)}, s32[96]{0:T(128)}, u32[]{:S(2)}) copy-start(s32[96]{0:T(128)} %param.18) | copy-start | bytes 1156
  307.1 4.9 copy-start.2
  329.9 4.9 copy-start.2
  352.7 4.9 copy-start.2
  375.4 4.9 copy-start.2
  398.2 4.9 copy-start.2
  421.0 4.9 copy-start.2
  437.1 0.7 copy-start.4
Sparse Core Ops, SparseCore 0:
  11.0 276.7 all-gather.1
  437.3 187.9 reduce-scatter.1
where the time goes:
time: 636 us; the launch traced here: 635 us
  waiting for transfers between devices  466 us (73%)
  local copies, waits for them, and re-layouts  90.8 us (14%)
  matrix products  41.9 us (7%)
  between operations  14.1 us (2%)
  other arithmetic  13.2 us (2%)
  loops' own time  9.02 us (1%)
    all_gather x1, waiting for transfers between devices, local(): every_eval = lax.all_gather(eval_tiles, 'corpus', axis=0, tiled=True)  279 us
    reduce_scatter x1, waiting for transfers between devices, local(): lax.psum_scatter(lax.fori_loop(0, groups, one_group, start_totals), 'voca...  186 us
    gather x6, local copies, waits for them, and re-layouts, compute(): eval_part = every_eval[eval_index]  63.2 us
    dot_general x6, matrix products, compute(): jnp.einsum('gij,gjrt->girt', matched.astype(jnp.bfloat16), corpus_part, p...  29.5 us
    gather x6, local copies, waits for them, and re-layouts, compute(): corpus_part = corpus_tiles[block_index]  15 us
  transfers between devices with their start and end apart: 2, of which 2 were waited for; matrix products, arithmetic and copies ran while one was open for 0% of the time, Pallas kernels for 0%

commit v1 on v0

--- a/solution.py
+++ b/solution.py
@@ -24,7 +24,9 @@
     tiles_slice = VOCAB // (term_width * slices)
     pair_slots = pair_eval_block.shape[0]
     quarter = pair_slots // slices
-    every_eval = lax.all_gather(eval_tiles, "corpus", axis=0, tiled=True)
+    every_eval = jnp.concatenate(
+        lax.all_to_all(jnp.stack([eval_tiles] * lax.axis_size("corpus")), "corpus", 0, 0), axis=0
+    )
     position = jnp.arange(pair_slots, dtype=jnp.int32)
     own_live = position < pair_count[0]
     groups = quarter * lax.axis_size("vocab") // GROUP

time: 636 us -> 1030 us (1.62)
  waiting for transfers between devices: 466 us -> 808 us
  matrix products: 41.9 us -> 71.6 us
  starting transfers between devices: 0.04 us -> 15.5 us
    all_to_all x0 -> x1, waiting for transfers between devices: none -> 592 us  [local(): lax.all_to_all(jnp.stack([eval_tiles] * lax.axis_size('corpus')), 'corpus...]
    all_gather x1 -> x0, waiting for transfers between devices: 279 us -> none  [local(): every_eval = lax.all_gather(eval_tiles, 'corpus', axis=0, tiled=True)]
    reduce_scatter x1, waiting for transfers between devices: 186 us -> 217 us  [local(): lax.psum_scatter(lax.fori_loop(0, groups, one_group, start_totals), 'voca...]
    dot_general x6, matrix products: 12.4 us -> 31.2 us  [compute(): jnp.einsum('girt,gist->grs', eval_part, aligned, preferred_element_type=j...]
    all_to_all x0 -> x1, starting transfers between devices: none -> 15.5 us  [local(): lax.all_to_all(jnp.stack([eval_tiles] * lax.axis_size('corpus')), 'corpus...]
    dot_general x6, matrix products: 29.5 us -> 40.4 us  [compute(): jnp.einsum('gij,gjrt->girt', matched.astype(jnp.bfloat16), corpus_part, p...]
where the time goes in v1:
time: 1030 us
  waiting for transfers between devices  808 us (78%)
  local copies, waits for them, and re-layouts  99.3 us (10%)
  matrix products  71.6 us (7%)
  starting transfers between devices  15.5 us (2%)
  between operations  14.1 us (1%)
  other arithmetic  13 us (1%)
    all_to_all x1, waiting for transfers between devices, local(): lax.all_to_all(jnp.stack([eval_tiles] * lax.axis_size('corpus')), 'corpus...  592 us
    reduce_scatter x1, waiting for transfers between devices, local(): lax.psum_scatter(lax.fori_loop(0, groups, one_group, start_totals), 'voca...  217 us
    gather x6, local copies, waits for them, and re-layouts, compute(): eval_part = every_eval[eval_index]  63.7 us
    dot_general x6, matrix products, compute(): jnp.einsum('gij,gjrt->girt', matched.astype(jnp.bfloat16), corpus_part, p...  40.4 us
    dot_general x6, matrix products, compute(): jnp.einsum('girt,gist->grs', eval_part, aligned, preferred_element_type=j...  31.2 us
  transfers between devices with their start and end apart: 2, of which 2 were waited for; matrix products, arithmetic and copies ran while one was open for 0% of the time, Pallas kernels for 0%

profile of v1, /device:TPU:1, one launch (start us, length us, event | category | flops | bytes accessed | tf_op | source)
XLA Modules:
  0.0 1030.1 jit_solution(9506784174704673060)
XLA Ops:
  6.5 9.4 stack.2
  16.0 15.5 %all-to-all-start = ((bf16[64,1,3,128,512]{4,3,2,1,0:T(8,128)(2,1)}), bf16[64,1,3,128,512]{4,3,2,1,0:T(8,128)(2,1)}, u32[]{:S(2)}, u32[]{:S(2)}) async-start(bf16[64,1,3,128,512]{4,3,2,1,0:T(8,128)(2,1)} %stack.2), calls=%async_computation | async-start | bytes 50331648 | tf_op jit(solution)/shard_map/all_to_all | solution.py:28
  32.2 0.1 copy.11
  32.3 591.5 %all-to-all-done = bf16[64,1,3,128,512]{4,3,2,1,0:T(8,128)(2,1)} async-done(((bf16[64,1,3,128,512]{4,3,2,1,0:T(8,128)(2,1)}), bf16[64,1,3,128,512]{4,3,2,1,0:T(8,128)(2,1)}, u32[]{:S(2)}, u32[]{:S(2)}) %all-to-all-start) | async-done | bytes 25165856 | tf_op jit(solution)/shard_map/all_to_all | solution.py:28
  623.8 3.5 broadcast_in_dim.49
  627.3 174.8 %while.16 = (s32[]{:T(128)}, f32[96,128,128]{2,1,0:T(8,128)}, pred[96]{0:T(512)(128)(4,1)S(1)}, s32[96]{0:T(128)S(1)}, bf16[64,3,128,512]{3,2,1,0:T(8,128)(2,1)}...) while((s32[]{:T(128)}, f32[96,128,128]{2,1,0:T(8,128)}, ...), condition=%wide.region_4.5_spmd, body=%wide.region_0.4_spmd.sunk | while | flops 412223712 | bytes 26748300 | solution.py:64
  627.3 0.8 fusion.15
  628.7 26.3 %conditional.2 = (f32[96,128,128]{2,1,0:T(8,128)}) conditional(s32[]{:T(128)} %convert_element_type.20, f32[96,128,128]{2,1,0:T(8,128)} %get-tuple-element.313, (pred[8]{0:T(512)(128)(4,1)S(1)}, s32[]{:T(128)}, s32[96]{0:T(128)S(1)}, bf16[64,3,128,512]{3,2,1,0:T(8,128)(2,1)}, s32[64,3]{1,0:T(8,128)S(1)}, /*index=5*/s32[96]{0:T(128)S(1)}, ...), branch_computations={%region_2.0_spmd, %region_3.3_spmd} | conditional | flops 412223712 | bytes 26748024 | solution.py:60
  628.8 0.6 gather_fusion.1
  629.4 2.5 gather_fusion.3
  631.9 0.6 gather_fusion.2
  632.4 6.7 fusion
  639.2 10.6 %gather_fusion = bf16[8,3,128,512]{3,2,1,0:T(8,128)(2,1)} fusion(bf16[64,3,128,512]{3,2,1,0:T(8,128)(2,1)} %get-tuple-element.178, s32[1024]{0:T(1024)S(1)} %pad_clamp_fusion.1), kind=kCustom, calls=%fused_computation | custom fusion | bytes 6291488 | tf_op jit(solution)/shard_map/while/body/eval_jaxpr/cond/branch_1_fun/gather | solution.py:41
  649.8 5.2 fusion.5
  655.0 0.8 fusion.15
  656.4 26.3 %conditional.2 = (f32[96,128,128]{2,1,0:T(8,128)}) conditional(s32[]{:T(128)} %convert_element_type.20, f32[96,128,128]{2,1,0:T(8,128)} %get-tuple-element.313, (pred[8]{0:T(512)(128)(4,1)S(1)}, s32[]{:T(128)}, s32[96]{0:T(128)S(1)}, bf16[64,3,128,512]{3,2,1,0:T(8,128)(2,1)}, s32[64,3]{1,0:T(8,128)S(1)}, /*index=5*/s32[96]{0:T(128)S(1)}, ...), branch_computations={%region_2.0_spmd, %region_3.3_spmd} | conditional | flops 412223712 | bytes 26748024 | solution.py:60
  656.5 0.6 gather_fusion.1
  657.1 2.5 gather_fusion.3
  659.6 0.6 gather_fusion.2
  660.1 6.7 fusion
  666.9 10.6 %gather_fusion = bf16[8,3,128,512]{3,2,1,0:T(8,128)(2,1)} fusion(bf16[64,3,128,512]{3,2,1,0:T(8,128)(2,1)} %get-tuple-element.178, s32[1024]{0:T(1024)S(1)} %pad_clamp_fusion.1), kind=kCustom, calls=%fused_computation | custom fusion | bytes 6291488 | tf_op jit(solution)/shard_map/while/body/eval_jaxpr/cond/branch_1_fun/gather | solution.py:41
  677.5 5.2 fusion.5
  682.7 0.8 fusion.15
  684.1 26.3 %conditional.2 = (f32[96,128,128]{2,1,0:T(8,128)}) conditional(s32[]{:T(128)} %convert_element_type.20, f32[96,128,128]{2,1,0:T(8,128)} %get-tuple-element.313, (pred[8]{0:T(512)(128)(4,1)S(1)}, s32[]{:T(128)}, s32[96]{0:T(128)S(1)}, bf16[64,3,128,512]{3,2,1,0:T(8,128)(2,1)}, s32[64,3]{1,0:T(8,128)S(1)}, /*index=5*/s32[96]{0:T(128)S(1)}, ...), branch_computations={%region_2.0_spmd, %region_3.3_spmd} | conditional | flops 412223712 | bytes 26748024 | solution.py:60
  684.2 0.6 gather_fusion.1
  684.8 2.5 gather_fusion.3
  687.2 0.6 gather_fusion.2
  687.8 6.7 fusion
  694.5 10.6 %gather_fusion = bf16[8,3,128,512]{3,2,1,0:T(8,128)(2,1)} fusion(bf16[64,3,128,512]{3,2,1,0:T(8,128)(2,1)} %get-tuple-element.178, s32[1024]{0:T(1024)S(1)} %pad_clamp_fusion.1), kind=kCustom, calls=%fused_computation | custom fusion | bytes 6291488 | tf_op jit(solution)/shard_map/while/body/eval_jaxpr/cond/branch_1_fun/gather | solution.py:41
  705.1 5.2 fusion.5
  710.3 0.8 fusion.15
  711.8 26.2 %conditional.2 = (f32[96,128,128]{2,1,0:T(8,128)}) conditional(s32[]{:T(128)} %convert_element_type.20, f32[96,128,128]{2,1,0:T(8,128)} %get-tuple-element.313, (pred[8]{0:T(512)(128)(4,1)S(1)}, s32[]{:T(128)}, s32[96]{0:T(128)S(1)}, bf16[64,3,128,512]{3,2,1,0:T(8,128)(2,1)}, s32[64,3]{1,0:T(8,128)S(1)}, /*index=5*/s32[96]{0:T(128)S(1)}, ...), branch_computations={%region_2.0_spmd, %region_3.3_spmd} | conditional | flops 412223712 | bytes 26748024 | solution.py:60
  711.9 0.6 gather_fusion.1
  712.5 2.5 gather_fusion.3
  714.9 0.6 gather_fusion.2
  715.5 6.7 fusion
  722.2 10.6 %gather_fusion = bf16[8,3,128,512]{3,2,1,0:T(8,128)(2,1)} fusion(bf16[64,3,128,512]{3,2,1,0:T(8,128)(2,1)} %get-tuple-element.178, s32[1024]{0:T(1024)S(1)} %pad_clamp_fusion.1), kind=kCustom, calls=%fused_computation | custom fusion | bytes 6291488 | tf_op jit(solution)/shard_map/while/body/eval_jaxpr/cond/branch_1_fun/gather | solution.py:41
  732.8 5.2 fusion.5
  738.0 0.8 fusion.15
  739.4 26.3 %conditional.2 = (f32[96,128,128]{2,1,0:T(8,128)}) conditional(s32[]{:T(128)} %convert_element_type.20, f32[96,128,128]{2,1,0:T(8,128)} %get-tuple-element.313, (pred[8]{0:T(512)(128)(4,1)S(1)}, s32[]{:T(128)}, s32[96]{0:T(128)S(1)}, bf16[64,3,128,512]{3,2,1,0:T(8,128)(2,1)}, s32[64,3]{1,0:T(8,128)S(1)}, /*index=5*/s32[96]{0:T(128)S(1)}, ...), branch_computations={%region_2.0_spmd, %region_3.3_spmd} | conditional | flops 412223712 | bytes 26748024 | solution.py:60
  739.5 0.6 gather_fusion.1
  740.1 2.5 gather_fusion.3
  742.6 0.6 gather_fusion.2
  743.1 6.7 fusion
  749.9 10.6 %gather_fusion = bf16[8,3,128,512]{3,2,1,0:T(8,128)(2,1)} fusion(bf16[64,3,128,512]{3,2,1,0:T(8,128)(2,1)} %get-tuple-element.178, s32[1024]{0:T(1024)S(1)} %pad_clamp_fusion.1), kind=kCustom, calls=%fused_computation | custom fusion | bytes 6291488 | tf_op jit(solution)/shard_map/while/body/eval_jaxpr/cond/branch_1_fun/gather | solution.py:41
  760.5 5.2 fusion.5
  765.7 0.8 fusion.15
  767.1 26.2 %conditional.2 = (f32[96,128,128]{2,1,0:T(8,128)}) conditional(s32[]{:T(128)} %convert_element_type.20, f32[96,128,128]{2,1,0:T(8,128)} %get-tuple-element.313, (pred[8]{0:T(512)(128)(4,1)S(1)}, s32[]{:T(128)}, s32[96]{0:T(128)S(1)}, bf16[64,3,128,512]{3,2,1,0:T(8,128)(2,1)}, s32[64,3]{1,0:T(8,128)S(1)}, /*index=5*/s32[96]{0:T(128)S(1)}, ...), branch_computations={%region_2.0_spmd, %region_3.3_spmd} | conditional | flops 412223712 | bytes 26748024 | solution.py:60
  767.2 0.6 gather_fusion.1
  767.8 2.5 gather_fusion.3
  770.2 0.6 gather_fusion.2
  770.8 6.7 fusion
  777.5 10.6 %gather_fusion = bf16[8,3,128,512]{3,2,1,0:T(8,128)(2,1)} fusion(bf16[64,3,128,512]{3,2,1,0:T(8,128)(2,1)} %get-tuple-element.178, s32[1024]{0:T(1024)S(1)} %pad_clamp_fusion.1), kind=kCustom, calls=%fused_computation | custom fusion | bytes 6291488 | tf_op jit(solution)/shard_map/while/body/eval_jaxpr/cond/branch_1_fun/gather | solution.py:41
  788.1 5.2 fusion.5
  793.3 0.8 fusion.15
  794.8 0.8 fusion.15
  796.2 0.8 fusion.15
  797.7 0.8 fusion.15
  799.2 0.8 fusion.15
  800.6 0.8 fusion.15
  802.3 0.6 gather_fusion.4
  802.9 0.6 gather_fusion.5
  803.4 216.8 %reduce-scatter.2.cloned.1.call-done = f32[24,128,128]{2,1,0:T(8,128)} async-done(((f32[96,128,128]{2,1,0:T(8,128)}), f32[24,128,128]{2,1,0:T(8,128)}) %reduce-scatter.2.cloned.1.call-update) | async-done | bytes 1572880 | tf_op jit(solution)/shard_map/reduce_scatter | solution.py:63
  1020.2 3.1 divide_select_fusion
  (51 shorter events, 0.9 us)
Async XLA Ops:
  6.5 795.7 %copy-start = (f32[8192]{0:T(1024)S(1)}, f32[8192]{0:T(1024)}, u32[]{:S(2)}) copy-start(f32[8192]{0:T(1024)} %param.20) | copy-start | bytes 98308
  16.0 16.2 %copy-start.6 = (s32[64,3]{0,1:T(4,128)S(1)}, s32[64,3]{0,1:T(4,128)}, u32[]{:S(2)}) copy-start(s32[64,3]{0,1:T(4,128)} %param.14) | copy-start | bytes 2308
  16.0 607.8 %all-to-all-start = ((bf16[64,1,3,128,512]{4,3,2,1,0:T(8,128)(2,1)}), bf16[64,1,3,128,512]{4,3,2,1,0:T(8,128)(2,1)}, u32[]{:S(2)}, u32[]{:S(2)}) async-start(bf16[64,1,3,128,512]{4,3,2,1,0:T(8,128)(2,1)} %stack.2), calls=%async_computation | async-start | bytes 50331648 | tf_op jit(solution)/shard_map/all_to_all | solution.py:28
  31.5 988.7 %reduce-scatter.2.cloned.1.call-start = ((), (), s32[]{:S(2)}) async-start(), calls=%async_computation.2 | async-start | bytes 7864320 | tf_op jit(solution)/shard_map/reduce_scatter | solution.py:63
  623.8 3.5 copy-start.1
  623.8 3.5 copy-start.2
  623.8 3.5 copy-start.4
  623.8 3.5 copy-start.5
  802.1 0.8 copy-start.3
Sparse Core Ops, SparseCore 0:
  802.2 217.9 reduce-scatter.1
